TPU v7x, 128 devices: a whole 4x4x4 slice. The times are simulated.
128 devices in a mesh: rep: 8 (over z_lo, x), tp: 16 (over y, z_hi, core).
Axes of the slice: x: 4, y: 4, z: 4 (z_hi: 2, z_lo: 2; z = z_hi * 2 + z_lo), core: 2. Of those that a mesh axis runs over, the one named last changes fastest.
Arguments:
- batch_rows: bfloat16 [12288, 4096], P(('rep', 'tp')), may hold values from -6 to 6
- token_slots: int32 [8, 384], P('rep'), may hold values from 0 to 1535, as said below
- holder_map: int32 [8, 16], P('rep'), may hold values from -2 to 111, as said below
- copies: bfloat16 [32768, 16384], P('rep', 'tp'), may hold values from -6 to 6
- upstream: bfloat16 [3072, 16384], P('rep', 'tp'), may hold values from -18 to 18
- up_act: bfloat16 [3072, 16384], P('rep', 'tp'), may hold values from -6 to 6
- master: float32 [4096, 14336], P('rep', 'tp'), may hold values from -0.078125 to 0.078125
- moment1: bfloat16 [4096, 14336], P('rep', 'tp'), may hold values from -0.75 to 0.75
- moment2: bfloat16 [4096, 14336], P('rep', 'tp'), may hold values from 0.049804688 to 2
Outputs:
- master_next: float32 [4096, 14336], P('rep', 'tp')
- moment1_next: bfloat16 [4096, 14336], P('rep', 'tp')
- moment2_next: bfloat16 [4096, 14336], P('rep', 'tp')
- copy_next: bfloat16 [32768, 16384], P('rep', 'tp')
Inputs may be any that keep to these rules, and one draw needn't show every extreme that they name: `token_slots`: row r lists 384 distinct rows of replica r's batch. `holder_map`: each row is one replica. A row is either -1 everywhere, or holds -2 at exactly 2 devices and at every other device a distinct piece 7 * j + s (0 <= s < 7) with j one of that row's -2 devices, each such piece exactly once. 4 rows are of the second kind. Columns of copies, upstream and up_act that the steps do not name are not read.
All inputs are finite; a program needn't handle non-finite values.
Results may differ from a plain program's by a relative error of at most 0.02.
Values may be sent and summed in bfloat16 or wider, within the bound.
A program may use at most 128 MiB of HBM per device.

v0:
```python
import math
import jax
import jax.numpy as jnp
from jax import lax
from jax.sharding import PartitionSpec as P

beta_one = 0.9
beta_two = 0.95
bias_one = 1.0 - 0.9**10
bias_two = 1.0 - 0.95**10
learn_rate = 0.05
weight_decay = 0.1
epsilon = 1e-08


def picked(indices, table):
    one_hot = (indices[:, None] == jnp.arange(table.shape[0], dtype=jnp.int32)[None, :]).astype(
        jnp.bfloat16
    )
    return jnp.dot(one_hot, table, preferred_element_type=jnp.float32).astype(jnp.bfloat16)


def on_device(
    batch_rows, token_slots, holder_map, copies, upstream, up_act, master, moment1, moment2
):
    tp_count = lax.axis_size("tp")
    rep_count = lax.axis_size("rep")
    position = lax.axis_index("tp")
    holders = holder_map[0]
    own_entry = jnp.sum(jnp.where(jnp.arange(tp_count) == position, holders, 0))
    all_holders = lax.all_gather(holders, "rep")
    unit_cols = copies.shape[1] // 8
    wide_cols = 7 * unit_cols
    scaling = 1.0 / math.sqrt(copies.shape[0])
    columns = lax.all_to_all(batch_rows, "tp", split_axis=1, concat_axis=0, tiled=True)
    chosen = picked(token_slots[0], columns)
    inputs = lax.all_gather(chosen, "tp", axis=1, tiled=True)
    gate_pre = jnp.dot(inputs, copies, preferred_element_type=jnp.float32) * scaling
    logistic = jax.nn.sigmoid(gate_pre)
    gate_grad = (
        upstream.astype(jnp.float32)
        * up_act.astype(jnp.float32)
        * logistic
        * (1.0 + gate_pre * (1.0 - logistic))
    ).astype(jnp.bfloat16)
    tokens = gate_grad.shape[0]
    pooled = lax.all_to_all(
        jnp.broadcast_to(gate_grad[:, wide_cols:], (tp_count, tokens, unit_cols)),
        "tp",
        split_axis=0,
        concat_axis=0,
        tiled=True,
    )
    wanted = position * 7 + jnp.arange(7, dtype=jnp.int32)
    choice = (holders[None, :] == wanted[:, None]).astype(jnp.bfloat16)
    rebuilt = jnp.concatenate(
        [
            jnp.sum(jnp.where(choice[s, :, None, None] > 0, pooled, jnp.zeros_like(pooled)), axis=0)
            for s in range(7)
        ],
        axis=1,
    )
    block_grad = jnp.where(own_entry == -2, rebuilt, gate_grad[:, :wide_cols])
    product = lax.dot_general(
        inputs, block_grad, (((0,), (0,)), ((), ())), preferred_element_type=jnp.float32
    )
    gradient = lax.psum_scatter(
        (product * scaling).astype(jnp.bfloat16), "rep", scatter_dimension=0, tiled=True
    ).astype(jnp.float32)
    first_new = beta_one * moment1.astype(jnp.float32) + (1.0 - beta_one) * gradient
    second_new = beta_two * moment2.astype(jnp.float32) + (1.0 - beta_two) * gradient * gradient
    step_size = first_new / bias_one / (jnp.sqrt(second_new / bias_two) + epsilon)
    master_next = master - learn_rate * (step_size + weight_decay * master)
    fresh = master_next.astype(jnp.bfloat16)
    full_block = lax.all_gather(fresh, "rep", axis=0, tiled=True)
    own_rows = fresh.shape[0]
    strip = own_rows // tp_count
    spread = lax.all_to_all(fresh, "tp", split_axis=0, concat_axis=0, tiled=True)
    table = spread.reshape(tp_count, strip, 7, unit_cols).transpose(0, 2, 1, 3)
    routed = picked(all_holders.reshape(-1), table.reshape(tp_count * 7, strip * unit_cols))
    routed = routed.reshape(rep_count, tp_count, strip, unit_cols)
    routed = lax.all_to_all(routed, "tp", split_axis=1, concat_axis=2, tiled=True)
    routed = routed.reshape(rep_count * own_rows, unit_cols)
    adopted = lax.all_to_all(routed, "rep", split_axis=0, concat_axis=0, tiled=True)
    copy_next = jnp.concatenate([full_block, adopted], axis=1)
    copy_next = jnp.where(own_entry == -2, jnp.zeros_like(copy_next), copy_next)
    return (master_next, first_new.astype(jnp.bfloat16), second_new.astype(jnp.bfloat16), copy_next)


def solution(mesh):
    placed = (
        P(("rep", "tp"), None),
        P("rep", None),
        P("rep", None),
        P("rep", "tp"),
        P("rep", "tp"),
        P("rep", "tp"),
        P("rep", "tp"),
        P("rep", "tp"),
        P("rep", "tp"),
    )
    return jax.shard_map(
        on_device,
        mesh=mesh,
        in_specs=placed,
        out_specs=(P("rep", "tp"), P("rep", "tp"), P("rep", "tp"), P("rep", "tp")),
        check_vma=False,
    )
```

profile of v0, /device:TPU:0, one launch (start us, length us, event | category | flops | bytes accessed | tf_op | source)
XLA Modules:
  0.0 366.0 jit_solution(13121369228132547831)
XLA Ops:
  7.2 2.1 copy.35
  9.3 8.1 %all-to-all-start = ((bf16[96,16,256]{2,0,1:T(8,128)(2,1)}), bf16[96,16,256]{2,0,1:T(8,128)(2,1)S(1)}, u32[]{:S(2)}, u32[]{:S(2)}) async-start(bf16[96,16,256]{2,0,1:T(8,128)(2,1)} %bitcast.40), calls=%async_computation | async-start | bytes 1572864 | tf_op jit(solution)/shard_map/all_to_all | solution.py:35
  17.4 0.0 all-gather.4.cloned.1.call-start
  17.5 15.1 %all-to-all-done = bf16[96,16,256]{2,0,1:T(8,128)(2,1)S(1)} async-done(((bf16[96,16,256]{2,0,1:T(8,128)(2,1)}), bf16[96,16,256]{2,0,1:T(8,128)(2,1)S(1)}, u32[]{:S(2)}, u32[]{:S(2)}) %all-to-all-start) | async-done | bytes 786464 | tf_op jit(solution)/shard_map/all_to_all | solution.py:35
  32.6 1.2 fusion.7
  33.8 51.7 %all-gather.4.cloned.1.call-done = bf16[384,4096]{1,0:T(8,128)(2,1)} async-done(((bf16[384,256]{1,0:T(8,128)(2,1)}), bf16[384,4096]{1,0:T(8,128)(2,1)}) %all-gather.4.cloned.1.call-update) | async-done | bytes 3145744 | tf_op jit(solution)/shard_map/all_gather | solution.py:37
  85.6 8.3 %multiply_convert_fusion.1 = bf16[384,1024]{1,0:T(8,128)(2,1)S(1)} fusion(bf16[384,1024]{1,0:T(8,128)(2,1)S(1)} %copy-done.5, bf16[384,1024]{1,0:T(8,128)(2,1)S(1)} %copy-done.6, bf16[384,4096]{1,0:T(8,128)(2,1)} %all-gather.4.cloned.1.call-done, bf16[4096,1024]{1,0:T(8,128)(2,1)} %param.12), kind=kOutput, calls=%fused_computation.17 | convolution fusion | flops 3226337280 | bytes 13893632 | tf_op jit(solution)/shard_map/dot_general | solution.py:38
  93.9 1.4 broadcast_in_dim.53
  95.3 3.9 %all-to-all-start.1 = ((bf16[16,384,128]{2,1,0:T(8,128)(2,1)}), bf16[16,384,128]{2,1,0:T(8,128)(2,1)S(1)}, u32[]{:S(2)}, u32[]{:S(2)}) async-start(bf16[16,384,128]{2,1,0:T(8,128)(2,1)} %broadcast_in_dim.53), calls=%async_computation.1 | async-start | bytes 3145728 | tf_op jit(solution)/shard_map/all_to_all | solution.py:47
  99.2 0.0 reduce-scatter.2.cloned.1.call-start
  99.3 0.6 fusion.12
  100.6 0.1 compare_convert_fusion
  100.6 22.1 %all-to-all-done.1 = bf16[16,384,128]{2,1,0:T(8,128)(2,1)S(1)} async-done(((bf16[16,384,128]{2,1,0:T(8,128)(2,1)}), bf16[16,384,128]{2,1,0:T(8,128)(2,1)S(1)}, u32[]{:S(2)}, u32[]{:S(2)}) %all-to-all-start.1) | async-done | bytes 1572896 | tf_op jit(solution)/shard_map/all_to_all | solution.py:47
  122.8 3.0 select_reduce_fusion
  126.0 6.4 %multiply_convert_fusion = bf16[4096,896]{1,0:T(8,128)(2,1)} fusion(bf16[384,4096]{1,0:T(8,128)(2,1)S(1)} %copy-done.4, bf16[384,896]{1,0:T(8,128)(2,1)S(1)} %constant_dynamic-update-slice_fusion, bf16[384,1024]{1,0:T(8,128)(2,1)S(1)} %multiply_convert_fusion.1, pred[]{:T(512)S(6)} %eq.59), kind=kOutput, calls=%fused_computation | convolution fusion | flops 2826256384 | bytes 11862017 | tf_op jit(solution)/shard_map/dot_general | solution.py:64
  132.5 81.7 %reduce-scatter.2.cloned.1.call-done = bf16[512,896]{1,0:T(8,128)(2,1)} async-done(((bf16[4096,896]{1,0:T(8,128)(2,1)}), bf16[512,896]{1,0:T(8,128)(2,1)}) %reduce-scatter.2.cloned.1.call-update) | async-done | bytes 917520 | tf_op jit(solution)/shard_map/reduce_scatter | solution.py:67
  214.3 5.7 %fusion.13 = (bf16[512,896]{1,0:T(8,128)(2,1)}, f32[512,896]{1,0:T(8,128)}, bf16[512,896]{1,0:T(8,128)(2,1)}, bf16[512,896]{1,0:T(8,128)(2,1)}) fusion(f32[512,896]{1,0:T(8,128)S(1)} %copy-done, bf16[512,896]{1,0:T(8,128)(2,1)S(1)} %copy-done.1, bf16[512,896]{1,0:T(8,128)(2,1)} %reduce-scatter.2.cloned.1.call-done, bf16[512,896]{1,0:T(8,128)(2,1)} %param.16), kind=kLoop, calls=%fused_computation.48 | loop fusion | flops 9633792 | bytes 9175040 | tf_op jit(solution)/shard_map/convert_element_type | solution.py:74
  220.0 6.7 %all-to-all-start.2 = ((bf16[16,32,896]{2,1,0:T(8,128)(2,1)}), bf16[16,32,896]{2,1,0:T(8,128)(2,1)S(1)}, u32[]{:S(2)}, u32[]{:S(2)}) async-start(bf16[16,32,896]{2,1,0:T(8,128)(2,1)} %bitcast.41), calls=%async_computation.3 | async-start | bytes 1835008 | tf_op jit(solution)/shard_map/all_to_all | solution.py:78
  226.7 20.7 %all-gather = s32[8,1,16]{2,1,0:T(1,128)S(1)} all-gather(s32[1,1,16]{2,1,0:T(1,128)S(1)} %bitcast.50), channel_id=1, replica_groups=mesh['rep'=8,'tp'=16] {'rep'}, dimensions={0}, use_global_device_ids=true | all-gather | bytes 576 | tf_op jit(solution)/shard_map/all_gather | solution.py:31
  247.4 0.6 broadcast.92
  248.0 0.7 reduce.11
  248.7 0.1 eq.63
  248.8 60.8 %all-to-all-done.2 = bf16[16,32,896]{2,1,0:T(8,128)(2,1)S(1)} async-done(((bf16[16,32,896]{2,1,0:T(8,128)(2,1)}), bf16[16,32,896]{2,1,0:T(8,128)(2,1)S(1)}, u32[]{:S(2)}, u32[]{:S(2)}) %all-to-all-start.2) | async-done | bytes 917536 | tf_op jit(solution)/shard_map/all_to_all | solution.py:78
  309.6 1.0 reshape.100
  310.6 0.2 copy.24
  310.8 0.5 fusion.5
  311.3 0.2 copy.29
  311.5 0.1 copy.25
  311.7 22.6 %all_to_all.54 = bf16[8,16,32,128]{3,2,0,1:T(8,128)(2,1)S(1)} all-to-all(bf16[8,16,32,128]{3,2,0,1:T(8,128)(2,1)S(1)} %copy.25), channel_id=1, replica_groups=mesh['rep'=8,'tp'=16] {'tp'}, dimensions={1} | all-to-all | bytes 2097152 | tf_op jit(solution)/shard_map/all_to_all | solution.py:82
  334.3 0.1 copy.26
  334.4 17.8 %all_to_all.55 = bf16[8,512,128]{2,1,0:T(8,128)(2,1)S(1)} all-to-all(bf16[8,512,128]{2,1,0:T(8,128)(2,1)S(1)} %bitcast.44), channel_id=1, replica_groups=mesh['rep'=8,'tp'=16] {'rep'}, dimensions={0} | all-to-all | bytes 2097152 | tf_op jit(solution)/shard_map/all_to_all | solution.py:84
  352.1 7.3 %maximum_select_fusion = bf16[4096,1024]{1,0:T(8,128)(2,1)} fusion(bf16[4096,128]{1,0:T(8,128)(2,1)S(1)} %bitcast.42, bf16[4096,896]{1,0:T(8,128)(2,1)} %all-gather.6.cloned.1.call-done, pred[]{:T(512)S(6)} %eq.59), kind=kLoop, calls=%fused_computation.1 | loop fusion | flops 20971520 | bytes 16777216 | tf_op jit(solution)/shard_map/jit(_where)/select_n | solution.py:86
  (30 shorter events, 0.4 us)
Async XLA Ops:
  7.2 10.3 %copy-start.3 = (s32[1,384]{1,0:T(1,128)S(1)}, s32[1,384]{1,0:T(1,128)}, u32[]{:S(2)}) copy-start(s32[1,384]{1,0:T(1,128)} %param.10) | copy-start | bytes 4612
  9.3 76.3 %copy-start.5 = (bf16[384,1024]{1,0:T(8,128)(2,1)S(1)}, bf16[384,1024]{1,0:T(8,128)(2,1)}, u32[]{:S(2)}) copy-start(bf16[384,1024]{1,0:T(8,128)(2,1)} %param.14) | copy-start | bytes 2359300
  9.3 76.3 %copy-start.6 = (bf16[384,1024]{1,0:T(8,128)(2,1)S(1)}, bf16[384,1024]{1,0:T(8,128)(2,1)}, u32[]{:S(2)}) copy-start(bf16[384,1024]{1,0:T(8,128)(2,1)} %param.13) | copy-start | bytes 2359300
  9.3 23.3 %all-to-all-start = ((bf16[96,16,256]{2,0,1:T(8,128)(2,1)}), bf16[96,16,256]{2,0,1:T(8,128)(2,1)S(1)}, u32[]{:S(2)}, u32[]{:S(2)}) async-start(bf16[96,16,256]{2,0,1:T(8,128)(2,1)} %bitcast.40), calls=%async_computation | async-start | bytes 1572864 | tf_op jit(solution)/shard_map/all_to_all | solution.py:35
  17.4 68.2 %all-gather.4.cloned.1.call-start = ((), (), s32[]{:S(2)}) async-start(), calls=%async_computation.6 | async-start | bytes 3342336 | tf_op jit(solution)/shard_map/all_gather | solution.py:37
  95.3 3.9 %copy-start.2 = (s32[1,16]{1,0:T(1,128)S(1)}, s32[1,16]{1,0:T(1,128)}, u32[]{:S(2)}) copy-start(s32[1,16]{1,0:T(1,128)} %param.11) | copy-start | bytes 196
  95.3 27.5 %all-to-all-start.1 = ((bf16[16,384,128]{2,1,0:T(8,128)(2,1)}), bf16[16,384,128]{2,1,0:T(8,128)(2,1)S(1)}, u32[]{:S(2)}, u32[]{:S(2)}) async-start(bf16[16,384,128]{2,1,0:T(8,128)(2,1)} %broadcast_in_dim.53), calls=%async_computation.1 | async-start | bytes 3145728 | tf_op jit(solution)/shard_map/all_to_all | solution.py:47
  99.2 115.1 %reduce-scatter.2.cloned.1.call-start = ((), (), s32[]{:S(2)}) async-start(), calls=%async_computation.7 | async-start | bytes 8257536 | tf_op jit(solution)/shard_map/reduce_scatter | solution.py:67
  122.8 3.2 copy-start.4
  132.4 81.8 %copy-start = (f32[512,896]{1,0:T(8,128)S(1)}, f32[512,896]{1,0:T(8,128)}, u32[]{:S(2)}) copy-start(f32[512,896]{1,0:T(8,128)} %param.15) | copy-start | bytes 5505028
  132.4 81.8 %copy-start.1 = (bf16[512,896]{1,0:T(8,128)(2,1)S(1)}, bf16[512,896]{1,0:T(8,128)(2,1)}, u32[]{:S(2)}) copy-start(bf16[512,896]{1,0:T(8,128)(2,1)} %param.17) | copy-start | bytes 2752516
  132.5 219.7 %all-gather.6.cloned.1.call-start = ((), (), s32[]{:S(2)}) async-start(), calls=%async_computation.8 | async-start | bytes 8257536 | tf_op jit(solution)/shard_map/all_gather | solution.py:75
  220.0 89.6 %all-to-all-start.2 = ((bf16[16,32,896]{2,1,0:T(8,128)(2,1)}), bf16[16,32,896]{2,1,0:T(8,128)(2,1)S(1)}, u32[]{:S(2)}, u32[]{:S(2)}) async-start(bf16[16,32,896]{2,1,0:T(8,128)(2,1)} %bitcast.41), calls=%async_computation.3 | async-start | bytes 1835008 | tf_op jit(solution)/shard_map/all_to_all | solution.py:78
Sparse Core Ops, SparseCore 0:
  33.9 51.5 all-gather.3
  132.6 81.6 reduce-scatter.1
  220.1 88.2 all-gather.5
where the time goes:
time: 367 us; the launch traced here: 366 us
  waiting for transfers between devices  232 us (63%)
  blocking collectives  61.1 us (17%)
  starting transfers between devices  18.8 us (5%)
  other arithmetic  17.5 us (5%)
  matrix products  16.4 us (4%)
  between operations  14.6 us (4%)
  local copies, waits for them, and re-layouts  6.07 us (2%)
    reduce_scatter x1, waiting for transfers between devices, on_device(): lax.psum_scatter((product * scaling).astype(jnp.bfloat16), 'rep', scatter...  81.7 us
    all_to_all x1, waiting for transfers between devices, on_device(): lax.all_to_all(fresh, 'tp', split_axis=0, concat_axis=0, tiled=True)  60.8 us
    all_gather x1, waiting for transfers between devices, on_device(): inputs = lax.all_gather(chosen, 'tp', axis=1, tiled=True)  51.7 us
    all_to_all x1, blocking collectives, on_device(): lax.all_to_all(routed, 'tp', split_axis=1, concat_axis=2, tiled=True)  22.6 us
    all_to_all x1, waiting for transfers between devices, on_device(): lax.all_to_all(jnp.broadcast_to(gate_grad[:, wide_cols:], (tp_count, toke...  22.1 us
    all_gather x1, blocking collectives, on_device(): all_holders = lax.all_gather(holders, 'rep')  20.7 us
    all_to_all x1, blocking collectives, on_device(): lax.all_to_all(routed, 'rep', split_axis=0, concat_axis=0, tiled=True)  17.8 us
    all_to_all x1, waiting for transfers between devices, on_device(): lax.all_to_all(batch_rows, 'tp', split_axis=1, concat_axis=0, tiled=True)  15.1 us
  transfers between devices with their start and end apart: 6, of which 5 were waited for; matrix products, arithmetic and copies ran while one was open for 1% of the time, Pallas kernels for 0%

commit v1 on v0

--- a/solution.py
+++ b/solution.py
@@ -34,7 +34,20 @@
     scaling = 1.0 / math.sqrt(copies.shape[0])
     columns = lax.all_to_all(batch_rows, "tp", split_axis=1, concat_axis=0, tiled=True)
     chosen = picked(token_slots[0], columns)
-    inputs = lax.all_gather(chosen, "tp", axis=1, tiled=True)
+
+    def pack_leaves(field_in):
+        r1 = jnp.concatenate(
+            lax.all_to_all(
+                jnp.stack([field_in for _ in range(lax.psum(1, axis_name="tp"))]),
+                "tp",
+                split_axis=0,
+                concat_axis=0,
+            ),
+            1,
+        )
+        return r1
+
+    inputs = pack_leaves(chosen)
     gate_pre = jnp.dot(inputs, copies, preferred_element_type=jnp.float32) * scaling
     logistic = jax.nn.sigmoid(gate_pre)
     gate_grad = (

time: 367 us -> 354 us (0.965)
  waiting for transfers between devices: 232 us -> 180 us
  blocking collectives: 61.1 us -> 104 us
  matrix products: 16.4 us -> 11.4 us
    all_gather x1 -> x0, waiting for transfers between devices: 51.7 us -> none  [on_device(): inputs = lax.all_gather(chosen, 'tp', axis=1, tiled=True)]
    all_to_all x0 -> x1, blocking collectives: none -> 43.5 us  [pack_leaves(): lax.all_to_all(jnp.stack([field_in for _ in range(lax.psum(1, axis_name='...]
    dot_general x1, matrix products: 8.27 us -> 3.95 us  [on_device(): jnp.dot(inputs, copies, preferred_element_type=jnp.float32) * scaling]
  transfers between devices with their start and end apart: 6 -> 5, of which waited for: 5 -> 4; matrix products, arithmetic and copies ran while one was open for 1% -> 1% of each run, Pallas kernels for 0% -> 0%
where the time goes in v1:
time: 354 us; the launch traced here: 353 us
  waiting for transfers between devices  180 us (51%)
  blocking collectives  104 us (29%)
  starting transfers between devices  18.6 us (5%)
  other arithmetic  17.5 us (5%)
  between operations  14.9 us (4%)
  matrix products  11.4 us (3%)
  local copies, waits for them, and re-layouts  6.64 us (2%)
    reduce_scatter x1, waiting for transfers between devices, on_device(): lax.psum_scatter((product * scaling).astype(jnp.bfloat16), 'rep', scatter...  81.4 us
    all_to_all x1, waiting for transfers between devices, on_device(): lax.all_to_all(fresh, 'tp', split_axis=0, concat_axis=0, tiled=True)  60.8 us
    all_to_all x1, blocking collectives, pack_leaves(): lax.all_to_all(jnp.stack([field_in for _ in range(lax.psum(1, axis_name='...  43.5 us
    all_to_all x1, blocking collectives, on_device(): lax.all_to_all(routed, 'tp', split_axis=1, concat_axis=2, tiled=True)  22.6 us
    all_to_all x1, waiting for transfers between devices, on_device(): lax.all_to_all(jnp.broadcast_to(gate_grad[:, wide_cols:], (tp_count, toke...  22.1 us
    all_gather x1, blocking collectives, on_device(): all_holders = lax.all_gather(holders, 'rep')  20.6 us
    all_to_all x1, blocking collectives, on_device(): lax.all_to_all(routed, 'rep', split_axis=0, concat_axis=0, tiled=True)  17.8 us
    all_to_all x1, waiting for transfers between devices, on_device(): lax.all_to_all(batch_rows, 'tp', split_axis=1, concat_axis=0, tiled=True)  15.1 us
  transfers between devices with their start and end apart: 5, of which 4 were waited for; matrix products, arithmetic and copies ran while one was open for 1% of the time, Pallas kernels for 0%

profile of v1, /device:TPU:0, one launch (start us, length us, event | category | flops | bytes accessed | tf_op | source)
XLA Modules:
  0.0 353.0 jit_solution(14420702355481920342)
XLA Ops:
  7.2 2.1 copy.40
  9.3 8.0 %all-to-all-start = ((bf16[96,16,256]{2,0,1:T(8,128)(2,1)}), bf16[96,16,256]{2,0,1:T(8,128)(2,1)S(1)}, u32[]{:S(2)}, u32[]{:S(2)}) async-start(bf16[96,16,256]{2,0,1:T(8,128)(2,1)} %bitcast.43), calls=%async_computation | async-start | bytes 1572864 | tf_op jit(solution)/shard_map/all_to_all | solution.py:35
  17.3 15.1 %all-to-all-done = bf16[96,16,256]{2,0,1:T(8,128)(2,1)S(1)} async-done(((bf16[96,16,256]{2,0,1:T(8,128)(2,1)}), bf16[96,16,256]{2,0,1:T(8,128)(2,1)S(1)}, u32[]{:S(2)}, u32[]{:S(2)}) %all-to-all-start) | async-done | bytes 786464 | tf_op jit(solution)/shard_map/all_to_all | solution.py:35
  32.4 0.6 fusion.7
  33.0 0.2 copy.28
  33.2 0.4 stack.2
  33.6 43.5 %all_to_all.59 = bf16[16,384,256]{1,2,0:T(8,128)(2,1)S(1)} all-to-all(bf16[16,384,256]{1,2,0:T(8,128)(2,1)S(1)} %stack.2), channel_id=1, replica_groups=mesh['rep'=8,'tp'=16] {'tp'}, dimensions={0} | all-to-all | bytes 6291456 | tf_op jit(solution)/shard_map/all_to_all | solution.py:40
  77.1 4.0 %multiply_convert_fusion.1 = bf16[384,1024]{1,0:T(8,128)(2,1)S(1)} fusion(bf16[384,1024]{1,0:T(8,128)(2,1)S(1)} %copy-done.7, bf16[384,1024]{1,0:T(8,128)(2,1)S(1)} %copy-done.8, bf16[384,4096]{0,1:T(8,128)(2,1)S(1)} %bitcast.50, bf16[4096,1024]{1,0:T(8,128)(2,1)S(1)} %copy-done.6), kind=kOutput, calls=%fused_computation.17 | convolution fusion | flops 3226337280 | bytes 13893632 | tf_op jit(solution)/shard_map/dot_general | solution.py:51
  81.1 1.4 broadcast_in_dim.53
  82.6 3.8 %all-to-all-start.2 = ((bf16[16,384,128]{2,1,0:T(8,128)(2,1)}), bf16[16,384,128]{2,1,0:T(8,128)(2,1)S(1)}, u32[]{:S(2)}, u32[]{:S(2)}) async-start(bf16[16,384,128]{2,1,0:T(8,128)(2,1)} %broadcast_in_dim.53), calls=%async_computation.2 | async-start | bytes 3145728 | tf_op jit(solution)/shard_map/all_to_all | solution.py:60
  86.5 0.6 fusion.12
  87.8 0.1 compare_convert_fusion
  87.9 22.1 %all-to-all-done.2 = bf16[16,384,128]{2,1,0:T(8,128)(2,1)S(1)} async-done(((bf16[16,384,128]{2,1,0:T(8,128)(2,1)}), bf16[16,384,128]{2,1,0:T(8,128)(2,1)S(1)}, u32[]{:S(2)}, u32[]{:S(2)}) %all-to-all-start.2) | async-done | bytes 1572896 | tf_op jit(solution)/shard_map/all_to_all | solution.py:60
  110.0 3.0 select_reduce_fusion
  113.2 6.4 %multiply_convert_fusion = bf16[4096,896]{1,0:T(8,128)(2,1)} fusion(bf16[384,4096]{0,1:T(8,128)(2,1)S(1)} %bitcast.51, bf16[384,896]{1,0:T(8,128)(2,1)S(1)} %constant_dynamic-update-slice_fusion, bf16[384,1024]{1,0:T(8,128)(2,1)S(1)} %multiply_convert_fusion.1, pred[]{:T(512)S(6)} %eq.59), kind=kOutput, calls=%fused_computation | convolution fusion | flops 2826256384 | bytes 11862017 | tf_op jit(solution)/shard_map/dot_general | solution.py:77
  119.7 81.4 %reduce-scatter.2.cloned.1.call-done = bf16[512,896]{1,0:T(8,128)(2,1)} async-done(((bf16[4096,896]{1,0:T(8,128)(2,1)}), bf16[512,896]{1,0:T(8,128)(2,1)}) %reduce-scatter.2.cloned.1.call-update) | async-done | bytes 917520 | tf_op jit(solution)/shard_map/reduce_scatter | solution.py:80
  201.0 5.7 %fusion.13 = (bf16[512,896]{1,0:T(8,128)(2,1)}, f32[512,896]{1,0:T(8,128)}, bf16[512,896]{1,0:T(8,128)(2,1)}, bf16[512,896]{1,0:T(8,128)(2,1)}) fusion(f32[512,896]{1,0:T(8,128)S(1)} %copy-done.2, bf16[512,896]{1,0:T(8,128)(2,1)S(1)} %copy-done.3, bf16[512,896]{1,0:T(8,128)(2,1)} %reduce-scatter.2.cloned.1.call-done, bf16[512,896]{1,0:T(8,128)(2,1)} %param.16), kind=kLoop, calls=%fused_computation.48 | loop fusion | flops 9633792 | bytes 9175040 | tf_op jit(solution)/shard_map/convert_element_type | solution.py:87
  206.8 6.7 %all-to-all-start.3 = ((bf16[16,32,896]{2,1,0:T(8,128)(2,1)}), bf16[16,32,896]{2,1,0:T(8,128)(2,1)S(1)}, u32[]{:S(2)}, u32[]{:S(2)}) async-start(bf16[16,32,896]{2,1,0:T(8,128)(2,1)} %bitcast.44), calls=%async_computation.4 | async-start | bytes 1835008 | tf_op jit(solution)/shard_map/all_to_all | solution.py:91
  213.5 20.6 %all-gather = s32[8,1,16]{2,1,0:T(1,128)S(1)} all-gather(s32[1,1,16]{2,1,0:T(1,128)S(1)} %bitcast.55), channel_id=1, replica_groups=mesh['rep'=8,'tp'=16] {'rep'}, dimensions={0}, use_global_device_ids=true | all-gather | bytes 576 | tf_op jit(solution)/shard_map/all_gather | solution.py:31
  234.1 0.6 broadcast.94
  234.7 0.7 reduce.11
  235.4 0.1 eq.63
  235.5 60.8 %all-to-all-done.3 = bf16[16,32,896]{2,1,0:T(8,128)(2,1)S(1)} async-done(((bf16[16,32,896]{2,1,0:T(8,128)(2,1)}), bf16[16,32,896]{2,1,0:T(8,128)(2,1)S(1)}, u32[]{:S(2)}, u32[]{:S(2)}) %all-to-all-start.3) | async-done | bytes 917536 | tf_op jit(solution)/shard_map/all_to_all | solution.py:91
  296.3 1.0 reshape.110
  297.4 0.2 copy.29
  297.5 0.5 fusion.5
  298.0 0.2 copy.34
  298.3 0.1 copy.30
  298.4 22.6 %all_to_all.60 = bf16[8,16,32,128]{3,2,0,1:T(8,128)(2,1)S(1)} all-to-all(bf16[8,16,32,128]{3,2,0,1:T(8,128)(2,1)S(1)} %copy.30), channel_id=1, replica_groups=mesh['rep'=8,'tp'=16] {'tp'}, dimensions={1} | all-to-all | bytes 2097152 | tf_op jit(solution)/shard_map/all_to_all | solution.py:95
  321.0 0.1 copy.31
  321.1 17.8 %all_to_all.61 = bf16[8,512,128]{2,1,0:T(8,128)(2,1)S(1)} all-to-all(bf16[8,512,128]{2,1,0:T(8,128)(2,1)S(1)} %bitcast.47), channel_id=1, replica_groups=mesh['rep'=8,'tp'=16] {'rep'}, dimensions={0} | all-to-all | bytes 2097152 | tf_op jit(solution)/shard_map/all_to_all | solution.py:97
  338.9 7.3 %maximum_select_fusion = bf16[4096,1024]{1,0:T(8,128)(2,1)} fusion(bf16[4096,128]{1,0:T(8,128)(2,1)S(1)} %bitcast.45, bf16[4096,896]{1,0:T(8,128)(2,1)} %all-gather.3.cloned.1.call-done, pred[]{:T(512)S(6)} %eq.59), kind=kLoop, calls=%fused_computation.1 | loop fusion | flops 20971520 | bytes 16777216 | tf_op jit(solution)/shard_map/jit(_where)/select_n | solution.py:99
  (34 shorter events, 0.4 us)
Async XLA Ops:
  7.2 10.1 %copy-start.5 = (s32[1,384]{1,0:T(1,128)S(1)}, s32[1,384]{1,0:T(1,128)}, u32[]{:S(2)}) copy-start(s32[1,384]{1,0:T(1,128)} %param.10) | copy-start | bytes 4612
  9.3 23.2 %all-to-all-start = ((bf16[96,16,256]{2,0,1:T(8,128)(2,1)}), bf16[96,16,256]{2,0,1:T(8,128)(2,1)S(1)}, u32[]{:S(2)}, u32[]{:S(2)}) async-start(bf16[96,16,256]{2,0,1:T(8,128)(2,1)} %bitcast.43), calls=%async_computation | async-start | bytes 1572864 | tf_op jit(solution)/shard_map/all_to_all | solution.py:35
  33.0 44.1 %copy-start.8 = (bf16[384,1024]{1,0:T(8,128)(2,1)S(1)}, bf16[384,1024]{1,0:T(8,128)(2,1)}, u32[]{:S(2)}) copy-start(bf16[384,1024]{1,0:T(8,128)(2,1)} %param.13) | copy-start | bytes 2359300
  33.2 43.9 %copy-start.6 = (bf16[4096,1024]{1,0:T(8,128)(2,1)S(1)}, bf16[4096,1024]{1,0:T(8,128)(2,1)}, u32[]{:S(2)}) copy-start(bf16[4096,1024]{1,0:T(8,128)(2,1)} %param.12) | copy-start | bytes 25165828
  33.6 43.5 %copy-start.7 = (bf16[384,1024]{1,0:T(8,128)(2,1)S(1)}, bf16[384,1024]{1,0:T(8,128)(2,1)}, u32[]{:S(2)}) copy-start(bf16[384,1024]{1,0:T(8,128)(2,1)} %param.14) | copy-start | bytes 2359300
  77.1 4.0 %copy-start = (bf16[16,384,256]{1,2,0:T(8,128)(2,1)}, bf16[16,384,256]{1,2,0:T(8,128)(2,1)S(1)}, u32[]{:S(2)}) copy-start(bf16[16,384,256]{1,2,0:T(8,128)(2,1)S(1)} %all_to_all.59) | copy-start | bytes 9437188
  82.6 3.9 %copy-start.4 = (s32[1,16]{1,0:T(1,128)S(1)}, s32[1,16]{1,0:T(1,128)}, u32[]{:S(2)}) copy-start(s32[1,16]{1,0:T(1,128)} %param.11) | copy-start | bytes 196
  82.6 27.4 %all-to-all-start.2 = ((bf16[16,384,128]{2,1,0:T(8,128)(2,1)}), bf16[16,384,128]{2,1,0:T(8,128)(2,1)S(1)}, u32[]{:S(2)}, u32[]{:S(2)}) async-start(bf16[16,384,128]{2,1,0:T(8,128)(2,1)} %broadcast_in_dim.53), calls=%async_computation.2 | async-start | bytes 3145728 | tf_op jit(solution)/shard_map/all_to_all | solution.py:60
  86.4 114.6 %reduce-scatter.2.cloned.1.call-start = ((), (), s32[]{:S(2)}) async-start(), calls=%async_computation.7 | async-start | bytes 8257536 | tf_op jit(solution)/shard_map/reduce_scatter | solution.py:80
  110.0 3.2 copy-start.1
  119.6 81.5 %copy-start.2 = (f32[512,896]{1,0:T(8,128)S(1)}, f32[512,896]{1,0:T(8,128)}, u32[]{:S(2)}) copy-start(f32[512,896]{1,0:T(8,128)} %param.15) | copy-start | bytes 5505028
  119.6 81.5 %copy-start.3 = (bf16[512,896]{1,0:T(8,128)(2,1)S(1)}, bf16[512,896]{1,0:T(8,128)(2,1)}, u32[]{:S(2)}) copy-start(bf16[512,896]{1,0:T(8,128)(2,1)} %param.17) | copy-start | bytes 2752516
  119.6 219.3 %all-gather.3.cloned.1.call-start = ((), (), s32[]{:S(2)}) async-start(), calls=%async_computation.8 | async-start | bytes 8257536 | tf_op jit(solution)/shard_map/all_gather | solution.py:88
  206.8 89.5 %all-to-all-start.3 = ((bf16[16,32,896]{2,1,0:T(8,128)(2,1)}), bf16[16,32,896]{2,1,0:T(8,128)(2,1)S(1)}, u32[]{:S(2)}, u32[]{:S(2)}) async-start(bf16[16,32,896]{2,1,0:T(8,128)(2,1)} %bitcast.44), calls=%async_computation.4 | async-start | bytes 1835008 | tf_op jit(solution)/shard_map/all_to_all | solution.py:91
Sparse Core Ops, SparseCore 0:
  119.7 81.2 reduce-scatter.1
  206.9 88.1 all-gather.2
